TPU v7x, 32 devices: a whole 2x2x4 slice. The times are simulated.
32 devices in a mesh: groups: 2 (over y), ctx: 8 (over z, x), mp: 2 (over core).
Axes of the slice: x: 2, y: 2, z: 4, core: 2. Of those that a mesh axis runs over, the one named last changes fastest.
Arguments:
- inputs: bfloat16 [2048, 2048], P(('groups', 'ctx'), 'mp'), parts along dimension 0, may hold values from -6 to 6
- cotangent: bfloat16 [2048, 2048], P(('groups', 'ctx'), 'mp'), parts along dimension 0, may hold values from -0.1875 to 0.1875
- filters: float32 [1024, 24], P('ctx'), may hold values from -0.1875 to 0.1875
- mixing: float32 [24, 2048], P(None, 'mp'), may hold values from -1.25 to 1.25
- ar_coef: float32 [3, 2048], P(None, 'mp'), may hold values from -3 to 3
Outputs:
- outputs: bfloat16 [2048, 2048], P(('groups', 'ctx'), 'mp'), parts along dimension 0
- grad_mixing: float32 [48, 2048], P('groups', 'mp'), parts along dimension 0
- grad_ar: float32 [6, 2048], P('groups', 'mp'), parts along dimension 0
There are 2 independent parts, one for each index of `groups`. A program takes and returns all parts, laid end to end along the dimension named above; an argument that names none is the same for every part. Nothing has to cross between parts.
All inputs are finite; a program needn't handle non-finite values.
Results may differ from a plain program's by a relative error of at most 0.001.
Values may be sent and summed in bfloat16 or wider, within the bound.
No kernel may reach another device: no remote copies, remote signals or barrier semaphores. Data moves between devices by JAX's collectives and lax.ppermute only.
A program may use at most 64 MiB of HBM per device.

v0:
```python
import math
import jax
import jax.numpy as jnp
from jax import lax
from jax.sharding import PartitionSpec as P

ORDER = 3
highest = lax.Precision.HIGHEST


def phase_tables(seq_len):
    radix_len = math.gcd(seq_len, 128)
    outer_len = 2 * seq_len // radix_len
    half_outer = outer_len // 2
    total_len = 2 * seq_len
    low_index = jnp.arange(half_outer, dtype=jnp.int32)
    outer_index = jnp.arange(outer_len, dtype=jnp.int32)
    radix_index = jnp.arange(radix_len, dtype=jnp.int32)
    outer_angle = (low_index[:, None] * outer_index[None, :] % outer_len).astype(jnp.float32) * (
        2.0 * math.pi / outer_len
    )
    twist_angle = (outer_index[:, None] * radix_index[None, :] % total_len).astype(jnp.float32) * (
        2.0 * math.pi / total_len
    )
    radix_angle = (radix_index[:, None] * radix_index[None, :] % radix_len).astype(jnp.float32) * (
        2.0 * math.pi / radix_len
    )
    return (
        jnp.cos(outer_angle),
        jnp.sin(outer_angle),
        jnp.cos(twist_angle),
        jnp.sin(twist_angle),
        jnp.cos(radix_angle),
        jnp.sin(radix_angle),
    )


def forward_spectrum(signal, tables):
    outer_cos, outer_sin, twist_cos, twist_sin, radix_cos, radix_sin = tables
    channels = signal.shape[0]
    folded = signal.reshape(channels, outer_cos.shape[0], radix_cos.shape[0])
    first_real = jnp.einsum("chr,hk->ckr", folded, outer_cos, precision=highest)
    first_imag = -jnp.einsum("chr,hk->ckr", folded, outer_sin, precision=highest)
    turned_real = first_real * twist_cos + first_imag * twist_sin
    turned_imag = first_imag * twist_cos - first_real * twist_sin
    spec_real = jnp.einsum("ckr,rq->ckq", turned_real, radix_cos, precision=highest) + jnp.einsum(
        "ckr,rq->ckq", turned_imag, radix_sin, precision=highest
    )
    spec_imag = jnp.einsum("ckr,rq->ckq", turned_imag, radix_cos, precision=highest) - jnp.einsum(
        "ckr,rq->ckq", turned_real, radix_sin, precision=highest
    )
    return (spec_real, spec_imag)


def inverse_spectrum(spec_real, spec_imag, tables):
    outer_cos, outer_sin, twist_cos, twist_sin, radix_cos, radix_sin = tables
    back_real = jnp.einsum("ckq,rq->ckr", spec_real, radix_cos, precision=highest) - jnp.einsum(
        "ckq,rq->ckr", spec_imag, radix_sin, precision=highest
    )
    back_imag = jnp.einsum("ckq,rq->ckr", spec_real, radix_sin, precision=highest) + jnp.einsum(
        "ckq,rq->ckr", spec_imag, radix_cos, precision=highest
    )
    untwist_real = back_real * twist_cos - back_imag * twist_sin
    untwist_imag = back_real * twist_sin + back_imag * twist_cos
    folded = jnp.einsum("ckr,hk->chr", untwist_real, outer_cos, precision=highest) - jnp.einsum(
        "ckr,hk->chr", untwist_imag, outer_sin, precision=highest
    )
    channels = folded.shape[0]
    total_len = 2 * folded.shape[1] * folded.shape[2]
    return folded.reshape(channels, -1) / total_len


def local(inputs, cotangent, filters, mixing, ar_coef):
    tok_rows, local_width = inputs.shape
    ctx_count = lax.axis_size("ctx")
    ctx_place = lax.axis_index("ctx")
    narrow = local_width // ctx_count
    seq_len = tok_rows * ctx_count
    tables = phase_tables(seq_len)
    seq_cols = lax.all_to_all(inputs.T, "ctx", split_axis=0, concat_axis=1, tiled=True)
    signal = seq_cols.astype(jnp.float32)
    filter_all = lax.all_gather(filters, "ctx", axis=0, tiled=True)
    mix_local = lax.dynamic_slice_in_dim(mixing, ctx_place * narrow, narrow, 1)
    kernel = jnp.einsum("lk,kc->cl", filter_all, mix_local, precision=highest)
    sig_real, sig_imag = forward_spectrum(signal, tables)
    ker_real, ker_imag = forward_spectrum(kernel, tables)
    convolved = inverse_spectrum(
        ker_real * sig_real - ker_imag * sig_imag, ker_real * sig_imag + ker_imag * sig_real, tables
    )
    cot_cols = lax.all_to_all(cotangent.T, "ctx", split_axis=0, concat_axis=1, tiled=True)
    cot_real, cot_imag = forward_spectrum(cot_cols.astype(jnp.float32), tables)
    lagged = inverse_spectrum(
        cot_real * sig_real + cot_imag * sig_imag, cot_imag * sig_real - cot_real * sig_imag, tables
    )
    ar_local = lax.dynamic_slice_in_dim(ar_coef, ctx_place * narrow, narrow, 1)
    padded = jnp.pad(signal, ((0, 0), (ORDER, 0)))
    autoreg = jnp.zeros_like(signal)
    for lag_step in range(1, ORDER + 1):
        autoreg = (
            autoreg
            + ar_local[lag_step - 1][:, None]
            * padded[:, ORDER - lag_step : ORDER - lag_step + seq_len]
        )
    out_cols = (convolved + autoreg).astype(jnp.bfloat16)
    outputs = lax.all_to_all(out_cols, "ctx", split_axis=1, concat_axis=0, tiled=True).T
    mix_piece = jnp.einsum("lk,cl->kc", filter_all, lagged, precision=highest)
    grad_mixing, grad_ar = (
        lax.all_gather(mix_piece, "ctx", axis=1, tiled=True),
        lax.all_gather(lagged[:, 1 : ORDER + 1].T, "ctx", axis=1, tiled=True),
    )
    return (outputs, grad_mixing, grad_ar)


def solution(mesh):
    return jax.shard_map(
        local,
        mesh=mesh,
        in_specs=(
            P(("groups", "ctx"), "mp"),
            P(("groups", "ctx"), "mp"),
            P("ctx", None),
            P(None, "mp"),
            P(None, "mp"),
        ),
        out_specs=(P(("groups", "ctx"), "mp"), P("groups", "mp"), P("groups", "mp")),
        check_vma=False,
    )
```

profile of v0, /device:TPU:0, one launch (start us, length us, event | category | flops | bytes accessed | tf_op | source)
XLA Modules:
  0.0 162.7 jit_solution(16318002603742689494)
XLA Ops:
  0.6 1.8 %copy.72 = bf16[128,1024]{0,1:T(8,128)(2,1)} copy(bf16[128,1024]{1,0:T(8,128)(2,1)} %param.5) | data formatting | bytes 524288 | tf_op args[0]
  2.5 7.3 %all-to-all-start = ((bf16[8,128,128]{2,1,0:T(8,128)(2,1)}), bf16[8,128,128]{2,1,0:T(8,128)(2,1)S(1)}, u32[]{:S(2)}, u32[]{:S(2)}) async-start(bf16[8,128,128]{2,1,0:T(8,128)(2,1)} %bitcast.7), calls=%async_computation | async-start | bytes 524288 | tf_op jit(solution)/shard_map/all_to_all | solution.py:80
  9.8 0.6 copy-done.3
  10.5 32.3 %all_gather.9 = f32[1024,24]{0,1:T(8,128)S(1)} all-gather(f32[128,24]{0,1:T(8,128)S(1)} %copy-done.3), channel_id=1, replica_groups=mesh['groups'=2,'ctx'=8,'mp'=2] {'ctx'}, dimensions={0}, use_global_device_ids=true | all-gather | bytes 110592 | tf_op jit(solution)/shard_map/all_gather | solution.py:82
  42.8 0.6 convolution_bitcast_fusion
  43.5 0.8 copy-done.2
  44.3 0.8 copy.84
  45.2 0.7 constant_dynamic-slice_fusion
  45.9 2.1 %convolution_negate_fusion = f32[16,128,128]{2,0,1:T(8,128)} fusion(f32[128,8,128]{2,1,0:T(8,128)S(1)} %bitcast.144), kind=kOutput, calls=%fused_computation | convolution fusion | flops 25429760 | bytes 1572864 | tf_op jit(solution)/shard_map/chr,hk->ckr/dot_general | solution.py:43
  47.9 4.8 %all-to-all-start.2 = ((bf16[8,128,128]{2,1,0:T(8,128)(2,1)}), bf16[8,128,128]{2,1,0:T(8,128)(2,1)S(1)}, u32[]{:S(2)}, u32[]{:S(2)}) async-start(bf16[8,128,128]{2,1,0:T(8,128)(2,1)} %bitcast.20), calls=%async_computation.2 | async-start | bytes 524288 | tf_op jit(solution)/shard_map/all_to_all | solution.py:90
  52.7 0.7 convolution_negate_fusion.2
  53.4 0.7 fusion.33
  54.1 6.3 %all-to-all-done.2 = bf16[8,128,128]{2,1,0:T(8,128)(2,1)S(1)} async-done(((bf16[8,128,128]{2,1,0:T(8,128)(2,1)}), bf16[8,128,128]{2,1,0:T(8,128)(2,1)S(1)}, u32[]{:S(2)}, u32[]{:S(2)}) %all-to-all-start.2) | async-done | bytes 262176 | tf_op jit(solution)/shard_map/all_to_all | solution.py:90
  60.4 0.7 convolution_negate_fusion.1
  61.1 0.7 fusion.30
  61.8 1.9 %add_bitcast_fusion = (f32[128,16,128]{2,1,0:T(8,128)S(1)}, f32[128,16,128]{2,1,0:T(8,128)S(1)}, f32[128,16,128]{2,1,0:T(8,128)S(1)}, f32[128,16,128]{2,1,0:T(8,...) fusion(f32[16,128,128]{2,0,1:T(8,128)S(1)} %convolution_negate_fusion.1, ...), kind=kOutput, calls=%fused_computation.30 | convolution fusion | flops 29886208 | bytes 12075008 | tf_op jit(solution)/shard_map/chr,hk->ckr/dot_general | solution.py:42
  63.7 1.4 fusion.24
  65.1 1.4 fusion.20
  66.6 1.4 convolution_add_fusion.4
  68.0 1.4 convolution_subtract_fusion.4
  69.5 1.4 fusion.18
  70.9 1.6 fusion.14
  72.5 1.4 convolution_add_fusion.3
  73.9 1.4 fusion.8
  75.4 1.4 fusion.12
  76.8 1.4 convolution_subtract_fusion.1
  78.3 1.4 convolution_subtract_fusion.3
  79.7 1.8 %multiply_subtract_fusion.1 = (f32[128,16,128]{2,0,1:T(8,128)S(1)}, f32[128,16,128]{2,0,1:T(8,128)S(1)}, f32[128,16,128]{2,0,1:T(8,128)S(1)}, f32[128,16,128]{2,0,1:T(8,128)S(1)}) fusion(f32[128,16,128]{2,0,1:T(8,128)S(1)} %convolution_subtract_fusion.3, f32[128,16,128]{2,0,1:T(8,128)S(1)} %convolution_subtract_fusion.1, ...), kind=kOutput, calls=%fused_computation.27 | convolution fusion | flops 406290432 | bytes 11534336 | tf_op jit(solution)/shard_map/ckr,rq->ckq/dot_general | solution.py:46
  81.5 1.2 fusion.58
  82.7 1.5 fusion.45
  84.2 1.2 fusion.53
  85.4 1.2 fusion.40
  86.7 1.3 convolution_subtract_fusion.2
  87.9 1.2 convolution_add_fusion.2
  89.2 1.2 convolution_subtract_fusion
  90.5 1.7 %multiply_add_fusion = (f32[128,16,128]{2,0,1:T(8,128)S(1)}, f32[128,16,128]{2,0,1:T(8,128)S(1)}, f32[128,16,128]{2,0,1:T(8,128)S(1)}, f32[128,16,128]{2,0,1:T(8,128)S(1)}) fusion(f32[128,16,128]{2,0,1:T(8,128)S(1)} %convolution_subtract_fusion, f32[16,128]{1,0:T(8,128)S(1)} %get-tuple-element.31, f32[16,128]{1,0:T(8,128)S(1)} %get-tuple-element.32, ...), kind=kOutput, calls=%fused_computation.25 | convolution fusion | flops 406290432 | bytes 9453568 | tf_op jit(solution)/shard_map/ckq,rq->ckr/dot_general | solution.py:60
  92.1 1.2 fusion.3
  93.3 1.2 fusion.6
  94.9 1.4 fusion.1
  96.8 0.8 copy.82
  97.6 3.4 %all-to-all-start.1 = ((bf16[128,8,128]{0,2,1:T(8,128)(2,1)}), bf16[128,8,128]{0,2,1:T(8,128)(2,1)S(1)}, u32[]{:S(2)}, u32[]{:S(2)}) async-start(bf16[128,8,128]{0,2,1:T(8,128)(2,1)} %bitcast.15), calls=%async_computation.1 | async-start | bytes 524288 | tf_op jit(solution)/shard_map/all_to_all | solution.py:105
  101.0 1.2 fusion
  102.5 26.6 %all_gather.11 = f32[3,1024]{1,0:T(4,128)S(1)} all-gather(f32[3,128]{1,0:T(4,128)S(1)} %bitcast.153), channel_id=1, replica_groups=mesh['groups'=2,'ctx'=8,'mp'=2] {'ctx'}, dimensions={1}, use_global_device_ids=true | all-gather | bytes 13824 | tf_op jit(solution)/shard_map/all_gather | solution.py:109
  129.1 0.5 convolution_bitcast_fusion.1
  129.6 30.6 %all_gather.10 = f32[24,1024]{1,0:T(8,128)S(1)} all-gather(f32[24,128]{1,0:T(8,128)S(1)} %convolution_bitcast_fusion.1), channel_id=1, replica_groups=mesh['groups'=2,'ctx'=8,'mp'=2] {'ctx'}, dimensions={1}, use_global_device_ids=true | all-gather | bytes 110592 | tf_op jit(solution)/shard_map/all_gather | solution.py:108
  160.4 0.9 copy.93
  161.2 0.6 copy.157
  161.9 0.6 copy.158
  (19 shorter events, 1.4 us)
Async XLA Ops:
  0.6 42.1 %copy-start = (f32[24,1024]{1,0:T(8,128)S(1)}, f32[24,1024]{1,0:T(8,128)}, u32[]{:S(2)}) copy-start(f32[24,1024]{1,0:T(8,128)} %param.8) | copy-start | bytes 294916
  2.5 45.4 %all-to-all-start = ((bf16[8,128,128]{2,1,0:T(8,128)(2,1)}), bf16[8,128,128]{2,1,0:T(8,128)(2,1)S(1)}, u32[]{:S(2)}, u32[]{:S(2)}) async-start(bf16[8,128,128]{2,1,0:T(8,128)(2,1)} %bitcast.7), calls=%async_computation | async-start | bytes 524288 | tf_op jit(solution)/shard_map/all_to_all | solution.py:80
  9.8 0.7 copy-start.3
  43.4 1.0 copy-start.2
  47.9 12.5 %all-to-all-start.2 = ((bf16[8,128,128]{2,1,0:T(8,128)(2,1)}), bf16[8,128,128]{2,1,0:T(8,128)(2,1)S(1)}, u32[]{:S(2)}, u32[]{:S(2)}) async-start(bf16[8,128,128]{2,1,0:T(8,128)(2,1)} %bitcast.20), calls=%async_computation.2 | async-start | bytes 524288 | tf_op jit(solution)/shard_map/all_to_all | solution.py:90
  60.4 1.4 copy-start.1
  97.6 62.6 %all-to-all-start.1 = ((bf16[128,8,128]{0,2,1:T(8,128)(2,1)}), bf16[128,8,128]{0,2,1:T(8,128)(2,1)S(1)}, u32[]{:S(2)}, u32[]{:S(2)}) async-start(bf16[128,8,128]{0,2,1:T(8,128)(2,1)} %bitcast.15), calls=%async_computation.1 | async-start | bytes 524288 | tf_op jit(solution)/shard_map/all_to_all | solution.py:105
where the time goes:
time: 166 us; the launch traced here: 163 us
  blocking collectives  89.5 us (54%)
  matrix products  41.1 us (25%)
  starting transfers between devices  15.5 us (9%)
  local copies, waits for them, and re-layouts  8.53 us (5%)
  waiting for transfers between devices  6.35 us (4%)
    all_gather x1, blocking collectives, local(): filter_all = lax.all_gather(filters, 'ctx', axis=0, tiled=True)  32.3 us
    all_gather x1, blocking collectives, local(): lax.all_gather(mix_piece, 'ctx', axis=1, tiled=True)  30.6 us
    all_gather x1, blocking collectives, local(): lax.all_gather(lagged[:, 1:ORDER + 1].T, 'ctx', axis=1, tiled=True)  26.6 us
    all_to_all x1, starting transfers between devices, local(): lax.all_to_all(inputs.T, 'ctx', split_axis=0, concat_axis=1, tiled=True)  7.28 us
    unnamed x17, local copies, waits for them, and re-layouts  6.57 us
    all_to_all x1, waiting for transfers between devices, local(): lax.all_to_all(cotangent.T, 'ctx', split_axis=0, concat_axis=1, tiled=True)  6.34 us
    all_to_all x1, starting transfers between devices, local(): lax.all_to_all(cotangent.T, 'ctx', split_axis=0, concat_axis=1, tiled=True)  4.76 us
    dot_general x3, matrix products, forward_spectrum(): jnp.einsum('ckr,rq->ckq', turned_imag, radix_sin, precision=highest)  4.67 us
  transfers between devices with their start and end apart: 3, of which 1 were waited for; matrix products, arithmetic and copies ran while one was open for 5% of the time, Pallas kernels for 0%

commit v1 on v0

--- a/solution.py
+++ b/solution.py
@@ -6,6 +6,22 @@
 
 ORDER = 3
 highest = lax.Precision.HIGHEST
+
+
+def gather_around(x, axis, dim):
+    ways, here, step = (lax.axis_size(axis), lax.axis_index(axis), x.shape[dim])
+    shape = [n * ways if d == dim else n for d, n in enumerate(x.shape)]
+    full = lax.dynamic_update_slice_in_dim(jnp.zeros(shape, x.dtype), x, here * step, axis=dim)
+    going_up = going_down = x
+    for far in range(1, ways // 2 + 1):
+        going_up = lax.ppermute(going_up, axis, [(d, (d + 1) % ways) for d in range(ways)])
+        full = lax.dynamic_update_slice_in_dim(full, going_up, (here - far) % ways * step, axis=dim)
+        if 2 * far < ways:
+            going_down = lax.ppermute(going_down, axis, [(d, (d - 1) % ways) for d in range(ways)])
+            full = lax.dynamic_update_slice_in_dim(
+                full, going_down, (here + far) % ways * step, axis=dim
+            )
+    return full
 
 
 def phase_tables(seq_len):
@@ -105,7 +121,7 @@
     outputs = lax.all_to_all(out_cols, "ctx", split_axis=1, concat_axis=0, tiled=True).T
     mix_piece = jnp.einsum("lk,cl->kc", filter_all, lagged, precision=highest)
     grad_mixing, grad_ar = (
-        lax.all_gather(mix_piece, "ctx", axis=1, tiled=True),
+        gather_around(mix_piece, "ctx", 1),
         lax.all_gather(lagged[:, 1 : ORDER + 1].T, "ctx", axis=1, tiled=True),
     )
     return (outputs, grad_mixing, grad_ar)

time: 166 us -> 161 us (0.970)
  blocking collectives: 89.5 us -> 58.2 us
  starting transfers between devices: 15.5 us -> 30.1 us
  waiting for transfers between devices: 6.35 us -> 18.2 us
    all_gather x1 -> x0, blocking collectives: 30.6 us -> none  [local(): lax.all_gather(mix_piece, 'ctx', axis=1, tiled=True)]
    ppermute x0 -> x7, starting transfers between devices: none -> 14.5 us  [the longest x3 12.5 us: gather_around(): lax.ppermute(going_down, axis, [(d, (d - 1) % ways) for d in range(ways)])]
    ppermute x0 -> x7, waiting for transfers between devices: none -> 11.9 us  [the longest x4 11.9 us: gather_around(): lax.ppermute(going_up, axis, [(d, (d + 1) % ways) for d in range(ways)])]
    unnamed x17 -> x18, local copies, waits for them, and re-layouts: 6.57 us -> 6.39 us
  transfers between devices with their start and end apart: 3 -> 10, of which waited for: 1 -> 4; matrix products, arithmetic and copies ran while one was open for 5% -> 6% of each run, Pallas kernels for 0% -> 0%
where the time goes in v1:
time: 161 us; the launch traced here: 158 us
  blocking collectives  58.2 us (36%)
  matrix products  40.9 us (25%)
  starting transfers between devices  30.1 us (19%)
  waiting for transfers between devices  18.2 us (11%)
  local copies, waits for them, and re-layouts  8.39 us (5%)
    all_gather x1, blocking collectives, local(): filter_all = lax.all_gather(filters, 'ctx', axis=0, tiled=True)  32.1 us
    all_gather x1, blocking collectives, local(): lax.all_gather(lagged[:, 1:ORDER + 1].T, 'ctx', axis=1, tiled=True)  26.1 us
    ppermute x3, starting transfers between devices, gather_around(): lax.ppermute(going_down, axis, [(d, (d - 1) % ways) for d in range(ways)])  12.5 us
    ppermute x4, waiting for transfers between devices, gather_around(): lax.ppermute(going_up, axis, [(d, (d + 1) % ways) for d in range(ways)])  11.9 us
    all_to_all x1, starting transfers between devices, local(): lax.all_to_all(inputs.T, 'ctx', split_axis=0, concat_axis=1, tiled=True)  7.28 us
    unnamed x18, local copies, waits for them, and re-layouts  6.39 us
    all_to_all x1, waiting for transfers between devices, local(): lax.all_to_all(cotangent.T, 'ctx', split_axis=0, concat_axis=1, tiled=True)  6.34 us
    all_to_all x1, starting transfers between devices, local(): lax.all_to_all(cotangent.T, 'ctx', split_axis=0, concat_axis=1, tiled=True)  4.93 us
  transfers between devices with their start and end apart: 10, of which 4 were waited for; matrix products, arithmetic and copies ran while one was open for 6% of the time, Pallas kernels for 0%

profile of v1, /device:TPU:0, one launch (start us, length us, event | category | flops | bytes accessed | tf_op | source)
XLA Modules:
  0.0 157.8 jit_solution(8714637921328216467)
XLA Ops:
  0.6 1.8 %copy.72 = bf16[128,1024]{0,1:T(8,128)(2,1)} copy(bf16[128,1024]{1,0:T(8,128)(2,1)} %param.5) | data formatting | bytes 524288 | tf_op args[0]
  2.5 7.3 %all-to-all-start = ((bf16[8,128,128]{2,1,0:T(8,128)(2,1)}), bf16[8,128,128]{2,1,0:T(8,128)(2,1)S(1)}, u32[]{:S(2)}, u32[]{:S(2)}) async-start(bf16[8,128,128]{2,1,0:T(8,128)(2,1)} %bitcast.7), calls=%async_computation | async-start | bytes 524288 | tf_op jit(solution)/shard_map/all_to_all | solution.py:96
  9.9 0.7 copy-done.4
  10.6 32.1 %all_gather.6 = f32[1024,24]{0,1:T(8,128)S(1)} all-gather(f32[128,24]{0,1:T(8,128)S(1)} %copy-done.4), channel_id=1, replica_groups=mesh['groups'=2,'ctx'=8,'mp'=2] {'ctx'}, dimensions={0}, use_global_device_ids=true | all-gather | bytes 110592 | tf_op jit(solution)/shard_map/all_gather | solution.py:98
  43.5 0.8 copy-done.2
  44.3 0.8 copy.84
  45.2 0.7 constant_dynamic-slice_fusion
  45.8 2.1 %convolution_negate_fusion = f32[16,128,128]{2,0,1:T(8,128)} fusion(f32[128,8,128]{2,1,0:T(8,128)S(1)} %bitcast.146), kind=kOutput, calls=%fused_computation | convolution fusion | flops 25429760 | bytes 1572864 | tf_op jit(solution)/shard_map/chr,hk->ckr/dot_general | solution.py:59
  47.9 4.9 %all-to-all-start.2 = ((bf16[8,128,128]{2,1,0:T(8,128)(2,1)}), bf16[8,128,128]{2,1,0:T(8,128)(2,1)S(1)}, u32[]{:S(2)}, u32[]{:S(2)}) async-start(bf16[8,128,128]{2,1,0:T(8,128)(2,1)} %bitcast.20), calls=%async_computation.2 | async-start | bytes 524288 | tf_op jit(solution)/shard_map/all_to_all | solution.py:106
  52.9 0.7 convolution_negate_fusion.2
  54.2 6.3 %all-to-all-done.2 = bf16[8,128,128]{2,1,0:T(8,128)(2,1)S(1)} async-done(((bf16[8,128,128]{2,1,0:T(8,128)(2,1)}), bf16[8,128,128]{2,1,0:T(8,128)(2,1)S(1)}, u32[]{:S(2)}, u32[]{:S(2)}) %all-to-all-start.2) | async-done | bytes 262176 | tf_op jit(solution)/shard_map/all_to_all | solution.py:106
  60.6 0.7 convolution_negate_fusion.1
  61.9 1.9 %add_bitcast_fusion = (f32[128,16,128]{2,1,0:T(8,128)S(1)}, f32[128,16,128]{2,1,0:T(8,128)S(1)}, f32[128,16,128]{2,1,0:T(8,128)S(1)}, f32[128,16,128]{2,1,0:T(8,...) fusion(f32[16,128,128]{2,0,1:T(8,128)S(1)} %convolution_negate_fusion.1, ...), kind=kOutput, calls=%fused_computation.30 | convolution fusion | flops 29886208 | bytes 12075008 | tf_op jit(solution)/shard_map/chr,hk->ckr/dot_general | solution.py:58
  63.9 1.4 fusion.24
  65.3 1.4 fusion.20
  66.7 1.4 convolution_add_fusion.4
  68.2 1.4 convolution_subtract_fusion.4
  69.6 1.4 fusion.18
  71.0 1.6 %fusion.14 = f32[128,16,128]{2,0,1:T(8,128)S(1)} fusion(f32[128,16,128]{2,1,0:T(8,128)S(1)} %get-tuple-element.24), kind=kOutput, calls=%fused_computation.45 | convolution fusion | flops 402882560 | bytes 2097152 | tf_op jit(solution)/shard_map/ckr,rq->ckq/dot_general | solution.py:65
  72.6 1.4 convolution_add_fusion.3
  74.1 1.4 fusion.8
  75.5 1.4 fusion.12
  77.0 1.4 convolution_subtract_fusion.1
  78.4 1.4 convolution_subtract_fusion.3
  79.9 1.8 %multiply_subtract_fusion.1 = (f32[128,16,128]{2,0,1:T(8,128)S(1)}, f32[128,16,128]{2,0,1:T(8,128)S(1)}, f32[128,16,128]{2,0,1:T(8,128)S(1)}, f32[128,16,128]{2,0,1:T(8,128)S(1)}) fusion(f32[128,16,128]{2,0,1:T(8,128)S(1)} %convolution_subtract_fusion.3, f32[128,16,128]{2,0,1:T(8,128)S(1)} %convolution_subtract_fusion.1, ...), kind=kOutput, calls=%fused_computation.27 | convolution fusion | flops 406290432 | bytes 11534336 | tf_op jit(solution)/shard_map/ckr,rq->ckq/dot_general | solution.py:62
  81.7 1.2 fusion.58
  82.9 1.5 fusion.45
  84.4 1.2 fusion.53
  85.6 1.2 fusion.40
  86.9 1.3 convolution_subtract_fusion.2
  88.1 1.2 convolution_add_fusion.2
  89.4 1.2 convolution_subtract_fusion
  90.6 1.7 %multiply_add_fusion = (f32[128,16,128]{2,0,1:T(8,128)S(1)}, f32[128,16,128]{2,0,1:T(8,128)S(1)}, f32[128,16,128]{2,0,1:T(8,128)S(1)}, f32[128,16,128]{2,0,1:T(8,128)S(1)}) fusion(f32[128,16,128]{2,0,1:T(8,128)S(1)} %convolution_subtract_fusion, f32[16,128]{1,0:T(8,128)S(1)} %get-tuple-element.33, f32[16,128]{1,0:T(8,128)S(1)} %get-tuple-element.34, ...), kind=kOutput, calls=%fused_computation.25 | convolution fusion | flops 406290432 | bytes 9453568 | tf_op jit(solution)/shard_map/ckq,rq->ckr/dot_general | solution.py:76
  92.3 1.2 fusion.3
  93.5 1.2 fusion
  95.3 4.9 %collective-permute-start.1 = (f32[24,128]{1,0:T(8,128)S(1)}, f32[24,128]{1,0:T(8,128)S(1)}, u32[]{:S(2)}, u32[]{:S(2)}) collective-permute-start(f32[24,128]{1,0:T(8,128)S(1)} %get-tuple-element.32), channel_id=1, source_target_pairs={{0,14},{2,0},{4,2},{6,4},{8,6},{10,8},{12,10},{14,12},{1,15},{3,1}... | collective-permute-start | bytes 36872 | tf_op jit(solution)/shard_map/ppermute | solution.py:20
  100.2 1.2 fusion.6
  101.8 1.2 fusion.1
  103.6 26.1 %all_gather.7 = f32[3,1024]{1,0:T(4,128)S(1)} all-gather(f32[3,128]{1,0:T(4,128)S(1)} %bitcast.155), channel_id=1, replica_groups=mesh['groups'=2,'ctx'=8,'mp'=2] {'ctx'}, dimensions={1}, use_global_device_ids=true | all-gather | bytes 13824 | tf_op jit(solution)/shard_map/all_gather | solution.py:125
  129.8 0.8 copy.82
  130.6 3.4 %all-to-all-start.1 = ((bf16[128,8,128]{0,2,1:T(8,128)(2,1)}), bf16[128,8,128]{0,2,1:T(8,128)(2,1)S(1)}, u32[]{:S(2)}, u32[]{:S(2)}) async-start(bf16[128,8,128]{0,2,1:T(8,128)(2,1)} %bitcast.15), calls=%async_computation.1 | async-start | bytes 524288 | tf_op jit(solution)/shard_map/all_to_all | solution.py:121
  134.0 1.9 %collective-permute-start.2 = (f32[24,128]{1,0:T(8,128)S(1)}, f32[24,128]{1,0:T(8,128)S(1)}, u32[]{:S(2)}, u32[]{:S(2)}) collective-permute-start(f32[24,128]{1,0:T(8,128)S(1)} %collective-permute-done), channel_id=1, source_target_pairs={{0,2},{2,4},{4,6},{6,8},{8,10},{10,12},{12,14},{14,0},{1,3},{3,5},... | collective-permute-start | bytes 36872 | tf_op jit(solution)/shard_map/ppermute | solution.py:17
  136.0 2.9 %collective-permute-start.3 = (f32[24,128]{1,0:T(8,128)S(1)}, f32[24,128]{1,0:T(8,128)S(1)}, u32[]{:S(2)}, u32[]{:S(2)}) collective-permute-start(f32[24,128]{1,0:T(8,128)S(1)} %collective-permute-done.1), channel_id=1, source_target_pairs={{0,14},{2,0},{4,2},{6,4},{8,6},{10,8},{12,10},{14,12},{1,15},{3,1}... | collective-permute-start | bytes 36872 | tf_op jit(solution)/shard_map/ppermute | solution.py:20
  138.8 3.8 %collective-permute-done.2 = f32[24,128]{1,0:T(8,128)S(1)} collective-permute-done((f32[24,128]{1,0:T(8,128)S(1)}, f32[24,128]{1,0:T(8,128)S(1)}, u32[]{:S(2)}, u32[]{:S(2)}) %collective-permute-start.2) | collective-permute-done | bytes 12320 | tf_op jit(solution)/shard_map/ppermute | solution.py:17
  142.7 4.7 %collective-permute-start.5 = (f32[24,128]{1,0:T(8,128)S(1)}, f32[24,128]{1,0:T(8,128)S(1)}, u32[]{:S(2)}, u32[]{:S(2)}) collective-permute-start(f32[24,128]{1,0:T(8,128)S(1)} %collective-permute-done.3), channel_id=1, source_target_pairs={{0,14},{2,0},{4,2},{6,4},{8,6},{10,8},{12,10},{14,12},{1,15},{3,1}... | collective-permute-start | bytes 36872 | tf_op jit(solution)/shard_map/ppermute | solution.py:20
  147.4 1.7 %collective-permute-done.4 = f32[24,128]{1,0:T(8,128)S(1)} collective-permute-done((f32[24,128]{1,0:T(8,128)S(1)}, f32[24,128]{1,0:T(8,128)S(1)}, u32[]{:S(2)}, u32[]{:S(2)}) %collective-permute-start.4) | collective-permute-done | bytes 12320 | tf_op jit(solution)/shard_map/ppermute | solution.py:17
  149.1 6.4 %collective-permute-done.6 = f32[24,128]{1,0:T(8,128)S(1)} collective-permute-done((f32[24,128]{1,0:T(8,128)S(1)}, f32[24,128]{1,0:T(8,128)S(1)}, u32[]{:S(2)}, u32[]{:S(2)}) %collective-permute-start.6) | collective-permute-done | bytes 12320 | tf_op jit(solution)/shard_map/ppermute | solution.py:17
  156.1 0.8 copy.93
  (41 shorter events, 5.0 us)
Async XLA Ops:
  0.6 42.1 %copy-start = (f32[24,1024]{1,0:T(8,128)S(1)}, f32[24,1024]{1,0:T(8,128)}, u32[]{:S(2)}) copy-start(f32[24,1024]{1,0:T(8,128)} %param.8) | copy-start | bytes 294916
  2.5 45.5 %all-to-all-start = ((bf16[8,128,128]{2,1,0:T(8,128)(2,1)}), bf16[8,128,128]{2,1,0:T(8,128)(2,1)S(1)}, u32[]{:S(2)}, u32[]{:S(2)}) async-start(bf16[8,128,128]{2,1,0:T(8,128)(2,1)} %bitcast.7), calls=%async_computation | async-start | bytes 524288 | tf_op jit(solution)/shard_map/all_to_all | solution.py:96
  9.9 0.7 copy-start.4
  43.4 1.0 copy-start.2
  47.9 12.6 %all-to-all-start.2 = ((bf16[8,128,128]{2,1,0:T(8,128)(2,1)}), bf16[8,128,128]{2,1,0:T(8,128)(2,1)S(1)}, u32[]{:S(2)}, u32[]{:S(2)}) async-start(bf16[8,128,128]{2,1,0:T(8,128)(2,1)} %bitcast.20), calls=%async_computation.2 | async-start | bytes 524288 | tf_op jit(solution)/shard_map/all_to_all | solution.py:106
  60.6 1.4 copy-start.1
  95.2 38.8 %collective-permute-start = (f32[24,128]{1,0:T(8,128)S(1)}, f32[24,128]{1,0:T(8,128)S(1)}, u32[]{:S(2)}, u32[]{:S(2)}) collective-permute-start(f32[24,128]{1,0:T(8,128)S(1)} %get-tuple-element.32), channel_id=1, source_target_pairs={{0,2},{2,4},{4,6},{6,8},{8,10},{10,12},{12,14},{14,0},{1,3},{3,5},... | collective-permute-start | bytes 36872 | tf_op jit(solution)/shard_map/ppermute | solution.py:17
  95.3 40.7 %collective-permute-start.1 = (f32[24,128]{1,0:T(8,128)S(1)}, f32[24,128]{1,0:T(8,128)S(1)}, u32[]{:S(2)}, u32[]{:S(2)}) collective-permute-start(f32[24,128]{1,0:T(8,128)S(1)} %get-tuple-element.32), channel_id=1, source_target_pairs={{0,14},{2,0},{4,2},{6,4},{8,6},{10,8},{12,10},{14,12},{1,15},{3,1}... | collective-permute-start | bytes 36872 | tf_op jit(solution)/shard_map/ppermute | solution.py:20
  130.6 24.9 %all-to-all-start.1 = ((bf16[128,8,128]{0,2,1:T(8,128)(2,1)}), bf16[128,8,128]{0,2,1:T(8,128)(2,1)S(1)}, u32[]{:S(2)}, u32[]{:S(2)}) async-start(bf16[128,8,128]{0,2,1:T(8,128)(2,1)} %bitcast.15), calls=%async_computation.1 | async-start | bytes 524288 | tf_op jit(solution)/shard_map/all_to_all | solution.py:121
  134.0 8.6 %collective-permute-start.2 = (f32[24,128]{1,0:T(8,128)S(1)}, f32[24,128]{1,0:T(8,128)S(1)}, u32[]{:S(2)}, u32[]{:S(2)}) collective-permute-start(f32[24,128]{1,0:T(8,128)S(1)} %collective-permute-done), channel_id=1, source_target_pairs={{0,2},{2,4},{4,6},{6,8},{8,10},{10,12},{12,14},{14,0},{1,3},{3,5},... | collective-permute-start | bytes 36872 | tf_op jit(solution)/shard_map/ppermute | solution.py:17
  136.0 6.7 %collective-permute-start.3 = (f32[24,128]{1,0:T(8,128)S(1)}, f32[24,128]{1,0:T(8,128)S(1)}, u32[]{:S(2)}, u32[]{:S(2)}) collective-permute-start(f32[24,128]{1,0:T(8,128)S(1)} %collective-permute-done.1), channel_id=1, source_target_pairs={{0,14},{2,0},{4,2},{6,4},{8,6},{10,8},{12,10},{14,12},{1,15},{3,1}... | collective-permute-start | bytes 36872 | tf_op jit(solution)/shard_map/ppermute | solution.py:20
  142.7 6.4 %collective-permute-start.4 = (f32[24,128]{1,0:T(8,128)S(1)}, f32[24,128]{1,0:T(8,128)S(1)}, u32[]{:S(2)}, u32[]{:S(2)}) collective-permute-start(f32[24,128]{1,0:T(8,128)S(1)} %collective-permute-done.2), channel_id=1, source_target_pairs={{0,2},{2,4},{4,6},{6,8},{8,10},{10,12},{12,14},{14,0},{1,3},{3,5},... | collective-permute-start | bytes 36872 | tf_op jit(solution)/shard_map/ppermute | solution.py:17
  142.7 6.4 %collective-permute-start.5 = (f32[24,128]{1,0:T(8,128)S(1)}, f32[24,128]{1,0:T(8,128)S(1)}, u32[]{:S(2)}, u32[]{:S(2)}) collective-permute-start(f32[24,128]{1,0:T(8,128)S(1)} %collective-permute-done.3), channel_id=1, source_target_pairs={{0,14},{2,0},{4,2},{6,4},{8,6},{10,8},{12,10},{14,12},{1,15},{3,1}... | collective-permute-start | bytes 36872 | tf_op jit(solution)/shard_map/ppermute | solution.py:20
  149.1 6.4 %collective-permute-start.6 = (f32[24,128]{1,0:T(8,128)S(1)}, f32[24,128]{1,0:T(8,128)S(1)}, u32[]{:S(2)}, u32[]{:S(2)}) collective-permute-start(f32[24,128]{1,0:T(8,128)S(1)} %collective-permute-done.4), channel_id=1, source_target_pairs={{0,2},{2,4},{4,6},{6,8},{8,10},{10,12},{12,14},{14,0},{1,3},{3,5},... | collective-permute-start | bytes 36872 | tf_op jit(solution)/shard_map/ppermute | solution.py:17
  155.5 0.6 copy-start.3
